TPU v7x, 32 devices: a whole 2x2x4 slice. The times are simulated.
32 devices in a mesh: band: 4 (over y, core), ga: 8 (over z, x).
Axes of the slice: x: 2, y: 2, z: 4, core: 2. Of those that a mesh axis runs over, the one named last changes fastest.
Arguments:
- density: float32 [160, 160, 160], P('ga'), may hold values from -6 to 6
- stick_column: int32 [20480], replicated, may hold values from 0 to 25599, as said below
- vloc: float32 [2, 160, 20480], P(None, None, 'ga'), may hold values from -0.0034179688 to 0.0034179688
- positions: float32 [3, 32], replicated, may hold values from 0 to 1
- species: int32 [32], replicated, may hold values from 0 to 1
- psi: bfloat16 [270336, 2, 1024], P('ga', None, 'band'), may hold values from -6 to 6
- miller_wave: int32 [3, 270336], P(None, 'ga'), may hold values from -40 to 40
- proj_radial: float32 [2, 8, 270336], P(None, None, 'ga'), may hold values from -0.01171875 to 0.01171875
- proj_count: int32 [2], replicated, may hold values from 4 to 8
- dcoef: float32 [2, 8, 8], replicated, may hold values from -0.0625 to 0.0625
- occupation: float32 [1024], P('band'), may hold values from 0 to 2
Outputs:
- density_sticks: float32 [2, 160, 20480], P(None, None, 'ga')
- forces: float32 [3, 32], replicated
Inputs may be any that keep to these rules, and one draw needn't show every extreme that they name: `stick_column`: distinct columns of the 160 by 160 frequency plane.
All inputs are finite; a program needn't handle non-finite values.
Results may differ from a plain program's by a relative error of at most 0.0036.
Values sent between devices are 32-bit elements; how exact they have to be, the bound alone decides.
A program may use at most 192 MiB of HBM per device.

v0:
```python
import math
import jax
import jax.numpy as jnp
from jax import lax
from jax.sharding import PartitionSpec as P

NX = 160
NY = 160
NZ = 160
TWO_PI = 2.0 * math.pi
EXACT = lax.Precision.HIGHEST


def frequency(index, count):
    return jnp.where(index >= count // 2, index - count, index)


def dft_table(count):
    index = jnp.arange(count, dtype=jnp.int32)
    angle = TWO_PI / count * (index[:, None] * index[None, :] % count).astype(jnp.float32)
    return (jnp.cos(angle), jnp.sin(angle))


def shards(
    density,
    stick_column,
    vloc,
    positions,
    species,
    psi,
    miller_wave,
    proj_radial,
    proj_count,
    dcoef,
    occupation,
):
    ga_index = lax.axis_index("ga")
    band_index = lax.axis_index("band")
    ga_count = lax.axis_size("ga")
    band_count = lax.axis_size("band")
    atom_count = positions.shape[1]
    kind_count = vloc.shape[0]
    slot_count = proj_radial.shape[1]
    sticks_here = vloc.shape[2]
    planes = density.shape[0]
    scale_norm = 1.0 / math.sqrt(NX * NY * NZ)
    start_zero = jnp.int32(0)
    cos_y, sin_y = dft_table(NY)
    cos_x, sin_x = dft_table(NX)
    batch_cos = jnp.broadcast_to(cos_x[None], (planes, NX, NX))
    batch_sin = jnp.broadcast_to(sin_x[None], (planes, NX, NX))
    xpass_real = jnp.einsum("pmx,pxy->pmy", batch_cos, density, precision=EXACT).reshape(
        planes * NX, NY
    )
    xpass_imag = -jnp.einsum("pmx,pxy->pmy", batch_sin, density, precision=EXACT).reshape(
        planes * NX, NY
    )
    full_real = jnp.dot(xpass_real, cos_y, precision=EXACT) + jnp.dot(
        xpass_imag, sin_y, precision=EXACT
    )
    full_imag = jnp.dot(xpass_imag, cos_y, precision=EXACT) - jnp.dot(
        xpass_real, sin_y, precision=EXACT
    )
    columns = jnp.concatenate(
        [full_real.reshape(planes, NX * NY), full_imag.reshape(planes, NX * NY)], axis=0
    )
    picked_rows = jnp.take(columns.T, stick_column, axis=0)
    chosen = picked_rows.T.reshape(2, planes, stick_column.shape[0])
    by_stick = lax.all_to_all(chosen, "ga", split_axis=2, concat_axis=1, tiled=True)
    cos_z, sin_z = dft_table(NZ)
    stick_real = (
        jnp.dot(cos_z, by_stick[0], precision=EXACT) + jnp.dot(sin_z, by_stick[1], precision=EXACT)
    ) * scale_norm
    stick_imag = (
        jnp.dot(cos_z, by_stick[1], precision=EXACT) - jnp.dot(sin_z, by_stick[0], precision=EXACT)
    ) * scale_norm
    density_sticks = jnp.stack([stick_real, stick_imag])
    owned = lax.dynamic_slice_in_dim(stick_column, ga_index * sticks_here, sticks_here)
    freq_x = frequency(owned // NY, NX).astype(jnp.float32)
    freq_y = frequency(owned % NY, NY).astype(jnp.float32)
    freq_z = frequency(jnp.arange(NZ, dtype=jnp.int32), NZ).astype(jnp.float32)
    wave_x = TWO_PI / NX * freq_x
    wave_y = TWO_PI / NY * freq_y
    wave_z = TWO_PI / NZ * freq_z
    per_band = atom_count // band_count
    band_start = band_index * per_band
    band_places = lax.dynamic_slice_in_dim(positions, band_start, per_band, 1)
    band_kinds = lax.dynamic_slice_in_dim(species, band_start, per_band)
    angle_plane = TWO_PI * (
        band_places[0][:, None] * freq_x[None, :] + band_places[1][:, None] * freq_y[None, :]
    )
    angle_depth = TWO_PI * band_places[2][:, None] * freq_z[None, :]
    channel_real = []
    channel_imag = []
    for kind_index in range(kind_count):
        base_real = vloc[kind_index] * stick_real
        base_imag = vloc[kind_index] * stick_imag
        for source, target in ((base_real, channel_real), (base_imag, channel_imag)):
            target.append(source * wave_x[None, :])
            target.append(source * wave_y[None, :])
            target.append(source * wave_z[:, None])
    field_real = jnp.stack(channel_real)
    field_imag = jnp.stack(channel_imag)
    plane_cos = jnp.cos(angle_plane)
    plane_sin = jnp.sin(angle_plane)
    summed_real = jnp.einsum("ak,qzk->aqz", plane_cos, field_real, precision=EXACT) - jnp.einsum(
        "ak,qzk->aqz", plane_sin, field_imag, precision=EXACT
    )
    summed_imag = jnp.einsum("ak,qzk->aqz", plane_cos, field_imag, precision=EXACT) + jnp.einsum(
        "ak,qzk->aqz", plane_sin, field_real, precision=EXACT
    )
    along_depth = jnp.sum(
        jnp.cos(angle_depth)[:, None, :] * summed_imag
        + jnp.sin(angle_depth)[:, None, :] * summed_real,
        axis=2,
    )
    along_depth = along_depth.reshape(per_band, kind_count, 3)
    band_pick = (band_kinds[:, None] == jnp.arange(kind_count, dtype=jnp.int32)[None, :]).astype(
        jnp.float32
    )
    local_part = jnp.einsum("asc,as->ca", along_depth, band_pick, precision=EXACT)
    local_full = lax.dynamic_update_slice(
        jnp.zeros((3, atom_count), jnp.float32), local_part, (start_zero, band_start)
    )
    local_total = lax.psum(local_full, ("band", "ga"))
    bands_here = psi.shape[2]
    waves_here = psi.shape[0]
    psi_flat = psi.reshape(waves_here, 2 * bands_here)
    miller_f = miller_wave.astype(jnp.float32)
    weights = jnp.stack(
        [
            jnp.ones_like(miller_f[0]),
            TWO_PI / NX * miller_f[0],
            TWO_PI / NY * miller_f[1],
            TWO_PI / NZ * miller_f[2],
        ]
    )

    def project_block(block_start, block_rows):
        block_atoms = block_rows // slot_count
        atom_start = block_start // slot_count
        block_places = lax.dynamic_slice_in_dim(positions, atom_start, block_atoms, 1)
        block_kinds = lax.dynamic_slice_in_dim(species, atom_start, block_atoms)
        phase = TWO_PI * (
            block_places[0][:, None] * miller_f[0][None, :]
            + block_places[1][:, None] * miller_f[1][None, :]
            + block_places[2][:, None] * miller_f[2][None, :]
        )
        radial = jnp.zeros((block_atoms, slot_count, waves_here), jnp.float32)
        for kind_index in range(kind_count):
            match = (block_kinds == kind_index).astype(jnp.float32)
            radial = radial + match[:, None, None] * proj_radial[kind_index][None]
        parts = jnp.stack(
            [radial * jnp.cos(phase)[:, None, :], radial * jnp.sin(phase)[:, None, :]], axis=2
        )
        table = (parts[:, :, None] * weights[None, None, :, None, :]).astype(jnp.bfloat16)
        product = jnp.dot(
            table.reshape(block_rows * 8, waves_here), psi_flat, preferred_element_type=jnp.float32
        )
        product = product.reshape(block_rows, 4, 2, 2, bands_here)
        proj_real = product[:, :, 0, 0] - product[:, :, 1, 1]
        proj_imag = product[:, :, 0, 1] + product[:, :, 1, 0]
        return jnp.stack([proj_real, proj_imag], axis=2).reshape(block_rows, 8 * bands_here)

    share_rows = atom_count * slot_count // ga_count
    block_rows = 64
    starts = block_rows * jnp.arange(
        share_rows * lax.axis_size("ga") // block_rows, dtype=jnp.int32
    )

    def one_block(block_start):
        return project_block(block_start, block_rows)

    owned_rows = lax.psum_scatter(
        lax.map(one_block, starts).reshape(share_rows * lax.axis_size("ga"), 8 * bands_here),
        "ga",
        scatter_dimension=0,
        tiled=True,
    )
    per_ga = share_rows // slot_count
    ga_start = ga_index * per_ga
    terms = owned_rows.reshape(per_ga, slot_count, 4, 2, bands_here)
    ga_kinds = lax.dynamic_slice_in_dim(species, ga_start, per_ga)
    ga_pick = (ga_kinds[:, None] == jnp.arange(kind_count, dtype=jnp.int32)[None, :]).astype(
        jnp.float32
    )
    live_slots = (jnp.arange(slot_count, dtype=jnp.int32)[None, :] < proj_count[:, None]).astype(
        jnp.float32
    )
    kind_table = dcoef * live_slots[:, :, None] * live_slots[:, None, :]
    coupling = jnp.einsum("as,sij->aij", ga_pick, kind_table, precision=EXACT)
    mixed_real = jnp.einsum("aij,ajcn->aicn", coupling, terms[:, :, 1:, 0], precision=EXACT)
    mixed_imag = jnp.einsum("aij,ajcn->aicn", coupling, terms[:, :, 1:, 1], precision=EXACT)
    value = (
        terms[:, :, 0, 0][:, :, None, :] * mixed_imag
        - terms[:, :, 0, 1][:, :, None, :] * mixed_real
    )
    nonlocal_part = 2.0 * jnp.einsum("aicn,n->ca", value, occupation, precision=EXACT)
    nonlocal_full = lax.dynamic_update_slice(
        jnp.zeros((3, atom_count), jnp.float32), nonlocal_part, (start_zero, ga_start)
    )
    forces = local_total + lax.psum(nonlocal_full, ("band", "ga"))
    return (density_sticks, forces)


def solution(mesh):
    in_specs = (
        P("ga", None, None),
        P(),
        P(None, None, "ga"),
        P(),
        P(),
        P("ga", None, "band"),
        P(None, "ga"),
        P(None, None, "ga"),
        P(),
        P(),
        P("band"),
    )
    out_specs = (P(None, None, "ga"), P())
    return jax.shard_map(shards, mesh=mesh, in_specs=in_specs, out_specs=out_specs, check_vma=False)
```

profile of v0, /device:TPU:0, one launch (start us, length us, event | category | flops | bytes accessed | tf_op | source)
XLA Modules:
  0.0 747.2 jit_solution(12256284340783067655)
XLA Ops:
  37.9 6.8 convolution_subtract_fusion
  56.0 9.0 %copy.65 = f32[40,25600]{0,1:T(8,128)} copy(f32[40,25600]{1,0:T(8,128)} %pad_maximum_fusion.2) | data formatting | bytes 8192000 | tf_op jit(solution)/shard_map/concatenate | solution.py:64
  65.0 73.2 %gather_fusion = f32[20480,40]{1,0:T(8,128)} fusion(f32[25600,40]{1,0:T(8,128)} %bitcast.221, s32[20480]{0:T(1024)S(1)} %fusion.53), kind=kCustom, calls=%fused_computation | custom fusion | bytes 6635520 | tf_op jit(solution)/shard_map/jit(_take)/gather | solution.py:67
  138.2 12.8 %select_bitcast_fusion = f32[40,20480]{0,1:T(8,128)} fusion(f32[20480,40]{1,0:T(8,128)} %gather_fusion, pred[20480]{0:T(1024)(128)(4,1)S(1)} %compare_and_fusion), kind=kLoop, calls=%fused_computation.31 | loop fusion | flops 819200 | bytes 6574080 | tf_op jit(solution)/shard_map/jit(_take)/select_n | solution.py:67
  150.9 20.9 %reshape.568 = f32[2,20,20480]{1,0,2:T(2,128)} reshape(f32[40,20480]{0,1:T(8,128)} %select_bitcast_fusion) | data formatting | bytes 6553600 | tf_op jit(solution)/shard_map/reshape | solution.py:68
  171.9 49.0 %reshape.570 = f32[8,1,102400]{2,1,0:T(1,128)} reshape(f32[20480,2,20]{2,1,0:T(2,128)} %bitcast.223) | data formatting | bytes 6553600
  220.9 7.4 all-to-all-start
  231.2 83.8 %copy.71 = bf16[33792,2,256]{0,2,1:T(8,128)(2,1)} copy(bf16[33792,2,256]{2,1,0:T(2,128)(2,1)} %param.18) | data formatting | bytes 69206016 | tf_op args[5]
  316.4 181.3 %while.12 = (s32[]{:T(128)}, f32[4,64,2048]{2,1,0:T(8,128)}, s32[4]{0:T(128)S(1)}, s32[32]{0:T(128)S(1)}, f32[2,8,33792]{2,1,0:T(8,128)}, /*index=5*/f32[3,32]{1...) while((s32[]{:T(128)}, f32[4,64,2048]{2,1,0:T(8,128)}, ...), condition=%wide.region_3.4_spmd, body=%wide.region_2.3_spmd.sunk | while | flops 17768366080 | bytes 125361648 | solution.py:175
  329.4 6.2 pad_maximum_fusion.7
  335.6 24.2 %fusion.149 = f32[64,4,2,2,256]{4,0,3,2,1:T(8,128)S(1)} fusion(bf16[2,256,33792,1,1]{2,1,0,4,3:T(8,128)(2,1)} %bitcast.227, f32[4,33792]{1,0:T(4,128)S(1)} %copy-done.11, f32[64,2,33792]{2,0,1:T(8,128)} %pad_maximum_fusion.7), kind=kOutput, calls=%fused_computation.3.clone.1 | convolution fusion | flops 17751343104 | bytes 53493760 | tf_op jit(solution)/shard_map/while/body/eval_jaxpr/dot_general | solution.py:157
  374.6 6.2 pad_maximum_fusion.7
  380.8 24.2 %fusion.149 = f32[64,4,2,2,256]{4,0,3,2,1:T(8,128)S(1)} fusion(bf16[2,256,33792,1,1]{2,1,0,4,3:T(8,128)(2,1)} %bitcast.227, f32[4,33792]{1,0:T(4,128)S(1)} %copy-done.11, f32[64,2,33792]{2,0,1:T(8,128)} %pad_maximum_fusion.7), kind=kOutput, calls=%fused_computation.3.clone.1 | convolution fusion | flops 17751343104 | bytes 53493760 | tf_op jit(solution)/shard_map/while/body/eval_jaxpr/dot_general | solution.py:157
  426.0 24.2 %fusion.149 = f32[64,4,2,2,256]{4,0,3,2,1:T(8,128)S(1)} fusion(bf16[2,256,33792,1,1]{2,1,0,4,3:T(8,128)(2,1)} %bitcast.227, f32[4,33792]{1,0:T(4,128)S(1)} %copy-done.11, f32[64,2,33792]{2,0,1:T(8,128)} %pad_maximum_fusion.7), kind=kOutput, calls=%fused_computation.3.clone.1 | convolution fusion | flops 17751343104 | bytes 53493760 | tf_op jit(solution)/shard_map/while/body/eval_jaxpr/dot_general | solution.py:157
  471.2 24.2 %fusion.149 = f32[64,4,2,2,256]{4,0,3,2,1:T(8,128)S(1)} fusion(bf16[2,256,33792,1,1]{2,1,0,4,3:T(8,128)(2,1)} %bitcast.227, f32[4,33792]{1,0:T(4,128)S(1)} %copy-done.11, f32[64,2,33792]{2,0,1:T(8,128)} %pad_maximum_fusion.7), kind=kOutput, calls=%fused_computation.3.clone.1 | convolution fusion | flops 17751343104 | bytes 53493760 | tf_op jit(solution)/shard_map/while/body/eval_jaxpr/dot_general | solution.py:157
  499.4 68.2 %reduce-scatter.2.cloned.1.call-done = f32[32,2048]{1,0:T(8,128)} async-done(((f32[256,2048]{1,0:T(8,128)}), f32[32,2048]{1,0:T(8,128)}) %reduce-scatter.2.cloned.1.call-update) | async-done | bytes 262160 | tf_op jit(solution)/shard_map/reduce_scatter | solution.py:174
  570.5 10.4 %reduce.2 = f32[8,102400]{1,0:T(8,128)S(1)} reduce(f32[8,1,102400]{2,1,0:T(1,128)} %all-to-all-done, f32[]{:T(128)} %broadcast.500), dimensions={1}, to_apply=%all_to_all.11.reduce_sub_computation | reduce | bytes 6553604 | tf_op jit(solution)/shard_map/all_to_all | solution.py:69
  580.9 42.1 %reshape.571 = f32[20480,2,20]{2,1,0:T(2,128)} reshape(f32[8,102400]{1,0:T(8,128)S(1)} %reduce.2) | data formatting | bytes 6553600
  623.0 16.8 %copy.87 = f32[2,20,8,2560]{3,2,0,1:T(8,128)S(1)} copy(f32[2,20,8,2560]{1,0,3,2:T(2,128)} %bitcast.224) | data formatting | bytes 6553600 | tf_op jit(solution)/shard_map/all_to_all | solution.py:69
  662.2 8.4 %fusion.31 = f32[8,6,160]{2,0,1:T(8,128)S(1)} fusion(f32[6,160,2560]{2,1,0:T(8,128)S(1)} %get-tuple-element.161, f32[2560]{0:T(1024)S(1)} %get-tuple-element.136, f32[8]{0:T(128)S(1)} %get-tuple-element.177, f32[2560]{0:T(1024)S(1)} %get-tuple-element.175, f32[8]{0:T(128)S(1)} %get-tuple-element.178), kind=kOutput, calls=%fused_computation.89 | convolution fusion | flops 236011520 | bytes 9881664 | tf_op jit(solution)/shard_map/ak,qzk->aqz/dot_general | solution.py:106
  670.6 8.3 %fusion.33 = f32[8,6,160]{2,0,1:T(8,128)S(1)} fusion(f32[6,160,2560]{2,1,0:T(8,128)S(1)} %get-tuple-element.162, f32[2560]{0:T(1024)S(1)} %get-tuple-element.136, f32[8]{0:T(128)S(1)} %get-tuple-element.177, f32[2560]{0:T(1024)S(1)} %get-tuple-element.175, f32[8]{0:T(128)S(1)} %get-tuple-element.178), kind=kOutput, calls=%fused_computation.91 | convolution fusion | flops 236011520 | bytes 9881664 | tf_op jit(solution)/shard_map/ak,qzk->aqz/dot_general | solution.py:109
  678.9 8.5 %fusion.20 = f32[8,6,160]{2,0,1:T(8,128)S(1)} fusion(f32[8,6,160]{2,0,1:T(8,128)S(1)} %fusion.33, f32[6,160,2560]{2,1,0:T(8,128)S(1)} %get-tuple-element.161, f32[2560]{0:T(1024)S(1)} %get-tuple-element.136, f32[8]{0:T(128)S(1)} %get-tuple-element.177, f32[2560]{0:T(1024)S(1)} %get-tuple-element.175, f32[8]{0:T(128)S(1)} %get-tuple-element.178, ...), kind=kOutput, calls=%fused_computation.68 | convolution fusion | flops 236026880 | bytes 9917504 | tf_op jit(solution)/shard_map/ak,qzk->aqz/dot_general | solution.py:109
  687.5 8.4 %fusion.21 = f32[8,6]{0,1:T(8,128)S(1)} fusion(f32[8,6,160]{2,0,1:T(8,128)S(1)} %fusion.20, f32[8,6,160]{2,0,1:T(8,128)S(1)} %fusion.31, f32[6,160,2560]{2,1,0:T(8,128)S(1)} %get-tuple-element.162, f32[2560]{0:T(1024)S(1)} %get-tuple-element.136, f32[8]{0:T(128)S(1)} %get-tuple-element.177, f32[2560]{0:T(1024)S(1)} %get-tuple-element.175, ...), kind=kOutput, calls=%fused_computation.69 | convolution fusion | flops 236042192 | bytes 9917696 | tf_op jit(solution)/shard_map/ak,qzk->aqz/dot_general | solution.py:106
  696.2 39.7 %psum.16 = f32[3,32]{1,0:T(4,128)} all-reduce(f32[3,32]{1,0:T(4,128)S(1)} %dynamic-update-slice), channel_id=1, replica_groups=mesh['band'=4,'ga'=8] {'band','ga'}, use_global_device_ids=true, to_apply=%region_1.2 | all-reduce | flops 96 | bytes 768 | tf_op jit(solution)/shard_map/psum | solution.py:125
  (182 shorter events, 139.5 us)
Async XLA Ops:
  7.2 3.1 copy-start
  13.4 7.0 copy-start.4
  32.3 5.6 copy-start.5
  220.9 7.5 %copy-start.12 = (s32[3,33792]{1,0:T(4,128)S(1)}, s32[3,33792]{1,0:T(4,128)}, u32[]{:S(2)}) copy-start(s32[3,33792]{1,0:T(4,128)} %param.19) | copy-start | bytes 1216516
  220.9 349.1 %all-to-all-start = ((f32[8,1,102400]{2,1,0:T(1,128)}), f32[8,1,102400]{2,1,0:T(1,128)}, u32[]{:S(2)}, u32[]{:S(2)}) async-start(f32[8,1,102400]{2,1,0:T(1,128)} %reshape.570), calls=%async_computation | async-start | bytes 6553600 | tf_op jit(solution)/shard_map/all_to_all | solution.py:69
  228.3 339.3 %reduce-scatter.2.cloned.1.call-start = ((), (), s32[]{:S(2)}) async-start(), calls=%async_computation.2 | async-start | bytes 2359296 | tf_op jit(solution)/shard_map/reduce_scatter | solution.py:174
  231.2 85.2 %copy-start.13 = (f32[3,32]{1,0:T(4,128)S(1)}, f32[3,32]{1,0:T(4,128)}, u32[]{:S(2)}) copy-start(f32[3,32]{1,0:T(4,128)} %param.16) | copy-start | bytes 1156
  231.2 85.1 %copy-start.14 = (s32[32]{0:T(128)S(1)}, s32[32]{0:T(128)}, u32[]{:S(2)}) copy-start(s32[32]{0:T(128)} %param.17) | copy-start | bytes 388
  316.4 181.7 %copy-start.17 = (s32[2]{0:T(128)S(1)}, s32[2]{0:T(128)}, u32[]{:S(2)}) copy-start(s32[2]{0:T(128)} %param.21) | copy-start | bytes 28
  316.4 181.8 %copy-start.15 = (f32[2,8,8]{2,1,0:T(8,128)S(1)}, f32[2,8,8]{2,1,0:T(8,128)}, u32[]{:S(2)}) copy-start(f32[2,8,8]{2,1,0:T(8,128)} %param.22) | copy-start | bytes 1540
  329.4 6.2 copy-start.11
  374.6 6.2 copy-start.11
  419.8 6.2 copy-start.11
  465.0 6.2 copy-start.11
  497.7 71.9 %copy-start.16 = (f32[256]{0:T(256)S(1)}, f32[256]{0:T(256)}, u32[]{:S(2)}) copy-start(f32[256]{0:T(256)} %param.23) | copy-start | bytes 3076
  643.4 5.1 copy-start.9
  645.1 5.6 copy-start.7
  652.7 2.2 copy-start.10
  654.9 2.3 copy-start.6
  654.9 2.4 copy-start.8
  657.2 4.5 copy-start.2
  659.8 1.9 copy-start.3
  735.9 4.0 copy-start.1
Sparse Core Ops, SparseCore 0:
  497.8 69.7 reduce-scatter.1
where the time goes:
time: 760 us; the launch traced here: 747 us
  local copies, waits for them, and re-layouts  346 us (46%)
  matrix products  168 us (22%)
  other arithmetic  92.7 us (12%)
  waiting for transfers between devices  68.2 us (9%)
  blocking collectives  39.7 us (5%)
  between operations  14.9 us (2%)
  loops' own time  9.85 us (1%)
    unnamed x39, local copies, waits for them, and re-layouts  175 us
    dot_general x4, matrix products, project_block(): jnp.dot(table.reshape(block_rows * 8, waves_here), psi_flat, preferred_el...  96.8 us
    gather x1, local copies, waits for them, and re-layouts, shards(): picked_rows = jnp.take(columns.T, stick_column, axis=0)  73.2 us
    reduce_scatter x1, waiting for transfers between devices, shards(): lax.psum_scatter(lax.map(one_block, starts).reshape(share_rows * lax.axis...  68.2 us
    psum x1, blocking collectives, shards(): local_total = lax.psum(local_full, ('band', 'ga'))  39.7 us
    another operation x4, other arithmetic, project_block(): jnp.stack([radial * jnp.cos(phase)[:, None, :], radial * jnp.sin(phase)[:...  24.7 us
    reshape x1, local copies, waits for them, and re-layouts, shards(): chosen = picked_rows.T.reshape(2, planes, stick_column.shape[0])  20.9 us
    all_to_all x2, local copies, waits for them, and re-layouts, shards(): lax.all_to_all(chosen, 'ga', split_axis=2, concat_axis=1, tiled=True)  17.3 us
  transfers between devices with their start and end apart: 2, of which 1 were waited for; matrix products, arithmetic and copies ran while one was open for 35% of the time, Pallas kernels for 0%

commit v1 on v0

--- a/solution.py
+++ b/solution.py
@@ -122,7 +122,7 @@
     local_full = lax.dynamic_update_slice(
         jnp.zeros((3, atom_count), jnp.float32), local_part, (start_zero, band_start)
     )
-    local_total = lax.psum(local_full, ("band", "ga"))
+    local_total = lax.psum(lax.psum(local_full, "ga"), "band")
     bands_here = psi.shape[2]
     waves_here = psi.shape[0]
     psi_flat = psi.reshape(waves_here, 2 * bands_here)

time: 760 us -> 788 us (1.037)
  blocking collectives: 39.7 us -> 66.4 us
    psum x1 -> x3, blocking collectives: 39.7 us -> 66.4 us  [the longest x1 40 us: shards(): forces = local_total + lax.psum(nonlocal_full, ('band', 'ga'))]
  transfers between devices with their start and end apart: 2 -> 2, of which waited for: 1 -> 1; matrix products, arithmetic and copies ran while one was open for 35% -> 34% of each run, Pallas kernels for 0% -> 0%
where the time goes in v1:
time: 788 us; the launch traced here: 775 us
  local copies, waits for them, and re-layouts  347 us (44%)
  matrix products  168 us (21%)
  other arithmetic  93.2 us (12%)
  waiting for transfers between devices  68.3 us (9%)
  blocking collectives  66.4 us (8%)
  between operations  14.9 us (2%)
  loops' own time  9.5 us (1%)
    unnamed x39, local copies, waits for them, and re-layouts  176 us
    dot_general x4, matrix products, project_block(): jnp.dot(table.reshape(block_rows * 8, waves_here), psi_flat, preferred_el...  96.8 us
    gather x1, local copies, waits for them, and re-layouts, shards(): picked_rows = jnp.take(columns.T, stick_column, axis=0)  73.2 us
    reduce_scatter x1, waiting for transfers between devices, shards(): lax.psum_scatter(lax.map(one_block, starts).reshape(share_rows * lax.axis...  68.2 us
    psum x1, blocking collectives, shards(): forces = local_total + lax.psum(nonlocal_full, ('band', 'ga'))  40 us
    psum x2, blocking collectives, shards(): local_total = lax.psum(lax.psum(local_full, 'ga'), 'band')  26.4 us
    another operation x4, other arithmetic, project_block(): jnp.stack([radial * jnp.cos(phase)[:, None, :], radial * jnp.sin(phase)[:...  24.7 us
    reshape x1, local copies, waits for them, and re-layouts, shards(): chosen = picked_rows.T.reshape(2, planes, stick_column.shape[0])  20.9 us
  transfers between devices with their start and end apart: 2, of which 1 were waited for; matrix products, arithmetic and copies ran while one was open for 34% of the time, Pallas kernels for 0%

profile of v1, /device:TPU:0, one launch (start us, length us, event | category | flops | bytes accessed | tf_op | source)
XLA Modules:
  0.0 775.3 jit_solution(11472524199174863709)
XLA Ops:
  37.9 6.8 convolution_subtract_fusion
  56.0 9.0 %copy.65 = f32[40,25600]{0,1:T(8,128)} copy(f32[40,25600]{1,0:T(8,128)} %pad_maximum_fusion.2) | data formatting | bytes 8192000 | tf_op jit(solution)/shard_map/concatenate | solution.py:64
  65.0 73.2 %gather_fusion = f32[20480,40]{1,0:T(8,128)} fusion(f32[25600,40]{1,0:T(8,128)} %bitcast.221, s32[20480]{0:T(1024)S(1)} %fusion.53), kind=kCustom, calls=%fused_computation | custom fusion | bytes 6635520 | tf_op jit(solution)/shard_map/jit(_take)/gather | solution.py:67
  138.2 12.8 %select_bitcast_fusion = f32[40,20480]{0,1:T(8,128)} fusion(f32[20480,40]{1,0:T(8,128)} %gather_fusion, pred[20480]{0:T(1024)(128)(4,1)S(1)} %compare_and_fusion), kind=kLoop, calls=%fused_computation.31 | loop fusion | flops 819200 | bytes 6574080 | tf_op jit(solution)/shard_map/jit(_take)/select_n | solution.py:67
  150.9 20.9 %reshape.568 = f32[2,20,20480]{1,0,2:T(2,128)} reshape(f32[40,20480]{0,1:T(8,128)} %select_bitcast_fusion) | data formatting | bytes 6553600 | tf_op jit(solution)/shard_map/reshape | solution.py:68
  171.9 50.3 %reshape.570 = f32[8,1,102400]{2,1,0:T(1,128)} reshape(f32[20480,2,20]{2,1,0:T(2,128)} %bitcast.223) | data formatting | bytes 6553600
  222.2 7.4 all-to-all-start
  232.5 83.8 %copy.71 = bf16[33792,2,256]{0,2,1:T(8,128)(2,1)} copy(bf16[33792,2,256]{2,1,0:T(2,128)(2,1)} %param.18) | data formatting | bytes 69206016 | tf_op args[5]
  317.6 180.8 %while.12 = (s32[]{:T(128)}, f32[4,64,2048]{2,1,0:T(8,128)}, s32[4]{0:T(128)S(1)}, s32[32]{0:T(128)S(1)}, f32[2,8,33792]{2,1,0:T(8,128)}, /*index=5*/f32[3,32]{1...) while((s32[]{:T(128)}, f32[4,64,2048]{2,1,0:T(8,128)}, ...), condition=%wide.region_4.5_spmd, body=%wide.region_3.4_spmd.sunk | while | flops 17768366080 | bytes 125361648 | solution.py:175
  336.8 24.2 %fusion.150 = f32[64,4,2,2,256]{4,0,3,2,1:T(8,128)S(1)} fusion(bf16[2,256,33792,1,1]{2,1,0,4,3:T(8,128)(2,1)} %bitcast.227, f32[4,33792]{1,0:T(4,128)S(1)} %copy-done.11, f32[64,2,33792]{2,0,1:T(8,128)} %pad_maximum_fusion.7), kind=kOutput, calls=%fused_computation.3.clone.1 | convolution fusion | flops 17751343104 | bytes 53493760 | tf_op jit(solution)/shard_map/while/body/eval_jaxpr/dot_general | solution.py:157
  382.0 24.2 %fusion.150 = f32[64,4,2,2,256]{4,0,3,2,1:T(8,128)S(1)} fusion(bf16[2,256,33792,1,1]{2,1,0,4,3:T(8,128)(2,1)} %bitcast.227, f32[4,33792]{1,0:T(4,128)S(1)} %copy-done.11, f32[64,2,33792]{2,0,1:T(8,128)} %pad_maximum_fusion.7), kind=kOutput, calls=%fused_computation.3.clone.1 | convolution fusion | flops 17751343104 | bytes 53493760 | tf_op jit(solution)/shard_map/while/body/eval_jaxpr/dot_general | solution.py:157
  421.0 6.2 pad_maximum_fusion.7
  427.2 24.2 %fusion.150 = f32[64,4,2,2,256]{4,0,3,2,1:T(8,128)S(1)} fusion(bf16[2,256,33792,1,1]{2,1,0,4,3:T(8,128)(2,1)} %bitcast.227, f32[4,33792]{1,0:T(4,128)S(1)} %copy-done.11, f32[64,2,33792]{2,0,1:T(8,128)} %pad_maximum_fusion.7), kind=kOutput, calls=%fused_computation.3.clone.1 | convolution fusion | flops 17751343104 | bytes 53493760 | tf_op jit(solution)/shard_map/while/body/eval_jaxpr/dot_general | solution.py:157
  472.4 24.2 %fusion.150 = f32[64,4,2,2,256]{4,0,3,2,1:T(8,128)S(1)} fusion(bf16[2,256,33792,1,1]{2,1,0,4,3:T(8,128)(2,1)} %bitcast.227, f32[4,33792]{1,0:T(4,128)S(1)} %copy-done.11, f32[64,2,33792]{2,0,1:T(8,128)} %pad_maximum_fusion.7), kind=kOutput, calls=%fused_computation.3.clone.1 | convolution fusion | flops 17751343104 | bytes 53493760 | tf_op jit(solution)/shard_map/while/body/eval_jaxpr/dot_general | solution.py:157
  500.2 68.2 %reduce-scatter.2.cloned.1.call-done = f32[32,2048]{1,0:T(8,128)} async-done(((f32[256,2048]{1,0:T(8,128)}), f32[32,2048]{1,0:T(8,128)}) %reduce-scatter.2.cloned.1.call-update) | async-done | bytes 262160 | tf_op jit(solution)/shard_map/reduce_scatter | solution.py:174
  570.9 40.0 %psum.23 = f32[3,32]{1,0:T(4,128)S(1)} all-reduce(f32[3,32]{1,0:T(4,128)S(1)} %dynamic_update_slice.14), channel_id=1, replica_groups=mesh['band'=4,'ga'=8] {'band','ga'}, use_global_device_ids=true, to_apply=%region_7.8 | all-reduce | flops 96 | bytes 768 | tf_op jit(solution)/shard_map/psum | solution.py:202
  611.5 10.4 %reduce.2 = f32[8,102400]{1,0:T(8,128)S(1)} reduce(f32[8,1,102400]{2,1,0:T(1,128)} %all-to-all-done, f32[]{:T(128)} %broadcast.500), dimensions={1}, to_apply=%all_to_all.11.reduce_sub_computation | reduce | bytes 6553604 | tf_op jit(solution)/shard_map/all_to_all | solution.py:69
  621.8 42.0 %reshape.571 = f32[20480,2,20]{2,1,0:T(2,128)} reshape(f32[8,102400]{1,0:T(8,128)S(1)} %reduce.2) | data formatting | bytes 6553600
  663.9 16.8 %copy.87 = f32[2,20,8,2560]{3,2,0,1:T(8,128)S(1)} copy(f32[2,20,8,2560]{1,0,3,2:T(2,128)} %bitcast.224) | data formatting | bytes 6553600 | tf_op jit(solution)/shard_map/all_to_all | solution.py:69
  703.1 8.4 %fusion.31 = f32[8,6,160]{2,0,1:T(8,128)S(1)} fusion(f32[6,160,2560]{2,1,0:T(8,128)S(1)} %get-tuple-element.161, f32[2560]{0:T(1024)S(1)} %get-tuple-element.136, f32[8]{0:T(128)S(1)} %get-tuple-element.177, f32[2560]{0:T(1024)S(1)} %get-tuple-element.175, f32[8]{0:T(128)S(1)} %get-tuple-element.178), kind=kOutput, calls=%fused_computation.89 | convolution fusion | flops 236011520 | bytes 9881664 | tf_op jit(solution)/shard_map/ak,qzk->aqz/dot_general | solution.py:106
  711.6 8.3 %fusion.33 = f32[8,6,160]{2,0,1:T(8,128)S(1)} fusion(f32[6,160,2560]{2,1,0:T(8,128)S(1)} %get-tuple-element.162, f32[2560]{0:T(1024)S(1)} %get-tuple-element.136, f32[8]{0:T(128)S(1)} %get-tuple-element.177, f32[2560]{0:T(1024)S(1)} %get-tuple-element.175, f32[8]{0:T(128)S(1)} %get-tuple-element.178), kind=kOutput, calls=%fused_computation.91 | convolution fusion | flops 236011520 | bytes 9881664 | tf_op jit(solution)/shard_map/ak,qzk->aqz/dot_general | solution.py:109
  719.9 8.5 %fusion.20 = f32[8,6,160]{2,0,1:T(8,128)S(1)} fusion(f32[8,6,160]{2,0,1:T(8,128)S(1)} %fusion.33, f32[6,160,2560]{2,1,0:T(8,128)S(1)} %get-tuple-element.161, f32[2560]{0:T(1024)S(1)} %get-tuple-element.136, f32[8]{0:T(128)S(1)} %get-tuple-element.177, f32[2560]{0:T(1024)S(1)} %get-tuple-element.175, f32[8]{0:T(128)S(1)} %get-tuple-element.178, ...), kind=kOutput, calls=%fused_computation.68 | convolution fusion | flops 236026880 | bytes 9917504 | tf_op jit(solution)/shard_map/ak,qzk->aqz/dot_general | solution.py:109
  728.4 8.4 %fusion.21 = f32[8,6]{0,1:T(8,128)S(1)} fusion(f32[8,6,160]{2,0,1:T(8,128)S(1)} %fusion.20, f32[8,6,160]{2,0,1:T(8,128)S(1)} %fusion.31, f32[6,160,2560]{2,1,0:T(8,128)S(1)} %get-tuple-element.162, f32[2560]{0:T(1024)S(1)} %get-tuple-element.136, f32[8]{0:T(128)S(1)} %get-tuple-element.177, f32[2560]{0:T(1024)S(1)} %get-tuple-element.175, ...), kind=kOutput, calls=%fused_computation.69 | convolution fusion | flops 236042192 | bytes 9917696 | tf_op jit(solution)/shard_map/ak,qzk->aqz/dot_general | solution.py:106
  737.0 20.8 %psum.21 = f32[3,32]{1,0:T(4,128)S(1)} all-reduce(f32[3,32]{1,0:T(4,128)S(1)} %dynamic_update_slice.13), channel_id=1, replica_groups=mesh['band'=4,'ga'=8] {'ga'}, use_global_device_ids=true, to_apply=%region_1.2 | all-reduce | flops 96 | bytes 768 | tf_op jit(solution)/shard_map/psum | solution.py:125
  (186 shorter events, 151.8 us)
Async XLA Ops:
  7.2 3.1 copy-start
  13.4 7.0 copy-start.4
  32.3 5.6 copy-start.5
  222.2 7.5 copy-start.12
  222.2 388.7 %all-to-all-start = ((f32[8,1,102400]{2,1,0:T(1,128)}), f32[8,1,102400]{2,1,0:T(1,128)}, u32[]{:S(2)}, u32[]{:S(2)}) async-start(f32[8,1,102400]{2,1,0:T(1,128)} %reshape.570), calls=%async_computation | async-start | bytes 6553600 | tf_op jit(solution)/shard_map/all_to_all | solution.py:69
  229.6 338.8 %reduce-scatter.2.cloned.1.call-start = ((), (), s32[]{:S(2)}) async-start(), calls=%async_computation.2 | async-start | bytes 2359296 | tf_op jit(solution)/shard_map/reduce_scatter | solution.py:174
  232.5 85.1 %copy-start.13 = (f32[3,32]{1,0:T(4,128)S(1)}, f32[3,32]{1,0:T(4,128)}, u32[]{:S(2)}) copy-start(f32[3,32]{1,0:T(4,128)} %param.16) | copy-start | bytes 1156
  232.5 85.1 %copy-start.14 = (s32[32]{0:T(128)S(1)}, s32[32]{0:T(128)}, u32[]{:S(2)}) copy-start(s32[32]{0:T(128)} %param.17) | copy-start | bytes 388
  317.6 181.3 %copy-start.17 = (s32[2]{0:T(128)S(1)}, s32[2]{0:T(128)}, u32[]{:S(2)}) copy-start(s32[2]{0:T(128)} %param.21) | copy-start | bytes 28
  317.6 181.4 %copy-start.15 = (f32[2,8,8]{2,1,0:T(8,128)S(1)}, f32[2,8,8]{2,1,0:T(8,128)}, u32[]{:S(2)}) copy-start(f32[2,8,8]{2,1,0:T(8,128)} %param.22) | copy-start | bytes 1540
  330.6 6.2 copy-start.11
  375.8 6.2 copy-start.11
  421.0 6.2 copy-start.11
  466.2 6.2 copy-start.11
  498.5 71.9 %copy-start.16 = (f32[256]{0:T(256)S(1)}, f32[256]{0:T(256)}, u32[]{:S(2)}) copy-start(f32[256]{0:T(256)} %param.23) | copy-start | bytes 3076
  684.3 5.1 copy-start.9
  686.0 5.6 copy-start.7
  693.6 2.2 copy-start.10
  695.8 2.3 copy-start.6
  695.8 2.4 copy-start.8
  698.1 4.5 copy-start.2
  700.7 1.9 copy-start.3
  764.0 4.0 copy-start.1
Sparse Core Ops, SparseCore 0:
  498.6 69.8 reduce-scatter.1
